TPU v7x, 512 devices: a whole 4x4x16 slice. The times are simulated.
512 devices in a mesh: row: 32 (over x, z_hi, core), col: 16 (over z_lo, y).
Axes of the slice: x: 4, y: 4, z: 16 (z_hi: 4, z_lo: 4; z = z_hi * 4 + z_lo), core: 2. Of those that a mesh axis runs over, the one named last changes fastest.
Arguments:
- top_inverse: float32 [2, 4096, 4096], P(None, 'row', 'col'), may hold values from -6 to 6
- panel: float32 [2, 2048, 8192], P(None, 'row', 'col'), may hold values from -0.09375 to 0.09375
- leaf_rows: int32 [32, 8], P('col'), may hold values from 0 to 15, as said below
- leaf_counts: int32 [32], P('col'), may hold values from 1 to 8, as said below
- diag_inverse: float32 [2, 256, 8192], P(None, 'row', 'col'), may hold values from -6 to 6
Outputs:
- selected: float32 [2, 4096, 8192], P(None, 'row', 'col')
- diagonal: float32 [2, 256, 8192], P(None, 'row', 'col')
Inputs may be any that keep to these rules, and one draw needn't show every extreme that they name: `leaf_rows`: the 8 entries of each leaf are distinct separator blocks. Slots 0 to leaf_counts - 1 of a leaf are live.
All inputs are finite; a program needn't handle non-finite values.
Results may differ from a plain program's by a relative error of at most 0.0003.
Values sent between devices are 32-bit elements; how exact they have to be, the bound alone decides.
A program may use at most 128 MiB of HBM per device.

v0:
```python
import jax
import jax.numpy as jnp
from jax import lax
from jax.sharding import PartitionSpec as P

B = 256
ROW_DEV = 128
LEAF_COL = 2


def product_highest(left, right):
    return jnp.dot(left, right, precision=lax.Precision.HIGHEST, preferred_element_type=jnp.float32)


def complex_product(left_real, left_imag, right_real, right_imag):
    real_part = product_highest(left_real, right_real) - product_highest(left_imag, right_imag)
    imag_part = product_highest(left_real, right_imag) + product_highest(left_imag, right_real)
    return (real_part, imag_part)


def on_device(top_inverse, panel, leaf_rows, leaf_counts, diag_inverse):
    slot_count = leaf_rows.shape[1]
    row_index = lax.axis_index("row")
    first_row = row_index * ROW_DEV
    my_block = first_row // B
    offset = first_row % B
    active_slots = jnp.arange(slot_count, dtype=jnp.int32)[None, :] < leaf_counts[:, None]
    block_live = jnp.any((leaf_rows == my_block) & active_slots, axis=1)
    targets = jnp.arange(ROW_DEV, dtype=jnp.int32)
    top_strip = lax.all_gather(top_inverse, "col", axis=2, tiled=True)
    section = lax.all_gather(panel, "row", axis=1, tiled=True)
    length = section.shape[1]
    gains_prod = []
    gains_low = []
    for absorb_member in range(LEAF_COL):
        position = jnp.arange(length, dtype=jnp.int32)
        slot_index = position // B
        slot_within = position % B
        slot_target_block = jnp.take(leaf_rows[absorb_member], slot_index)
        slot_active = slot_index < leaf_counts[absorb_member]
        columns = slot_target_block * B + slot_within
        panel_part = (
            section[:, :, absorb_member * B : (absorb_member + 1) * B]
            * slot_active.astype(jnp.float32)[None, :, None]
        )
        picked = jnp.take(top_strip, columns, axis=2)
        real_part, imag_part = complex_product(picked[0], picked[1], panel_part[0], panel_part[1])
        gain_prod = jnp.stack([real_part, imag_part])
        owned = slot_active & (slot_target_block == my_block)
        select = ((slot_within[None, :] - offset == targets[:, None]) & owned[None, :]).astype(
            jnp.float32
        )
        gain_low = jnp.stack(
            [product_highest(select, panel_part[0]), product_highest(select, panel_part[1])]
        )
        gains_prod.append(gain_prod)
        gains_low.append(gain_low)
    product = jnp.concatenate(gains_prod, axis=2)
    lower_rows = jnp.concatenate(gains_low, axis=2)
    keep_rows = jnp.repeat(block_live.astype(jnp.float32), B)
    selected = -product * keep_rows[None, None, :]
    diag_parts = []
    for member in range(LEAF_COL):
        sel_block = selected[:, :, member * B : (member + 1) * B]
        low_block = lower_rows[:, :, member * B : (member + 1) * B]
        diag_real, diag_imag = complex_product(
            sel_block[0].T, sel_block[1].T, low_block[0], low_block[1]
        )
        diag_parts.append(jnp.stack([diag_real, diag_imag]))
    partial_diag = jnp.concatenate(diag_parts, axis=2)
    total_sum = lax.psum(partial_diag, "row")
    share_rows = diag_inverse.shape[1]
    share_sum = lax.dynamic_slice_in_dim(total_sum, row_index * share_rows, share_rows, 1)
    return (selected, diag_inverse - share_sum)


def solution(mesh):
    return jax.shard_map(
        on_device,
        mesh=mesh,
        in_specs=(
            P(None, "row", "col"),
            P(None, "row", "col"),
            P("col", None),
            P("col"),
            P(None, "row", "col"),
        ),
        out_specs=(P(None, "row", "col"), P(None, "row", "col")),
        check_vma=False,
    )
```

profile of v0, /device:TPU:1, one launch (start us, length us, event | category | flops | bytes accessed | tf_op | source)
XLA Modules:
  0.0 626.7 jit_solution(4336711945029545441)
XLA Ops:
  7.2 1.8 copy.12
  12.3 5.2 compare_and_fusion.1
  18.8 5.7 compare_and_fusion.3
  24.5 4.9 compare_and_fusion
  29.4 5.5 compare_and_fusion.2
  35.0 4.9 broadcast_clamp_fusion
  39.9 5.2 broadcast_clamp_fusion.1
  46.3 52.9 %all-gather.3.cloned.1.call-done = f32[2,128,4096]{1,0,2:T(2,128)} async-done(((f32[2,128,256]{1,0,2:T(2,128)}), f32[2,128,4096]{1,0,2:T(2,128)}) %all-gather.3.cloned.1.call-update) | async-done | bytes 4194320 | tf_op jit(solution)/shard_map/all_gather | solution.py:30
  99.2 9.0 %gather_fusion.1 = f32[2048,2,128]{2,1,0:T(2,128)S(1)} fusion(f32[2,128,4096]{1,0,2:T(2,128)} %all-gather.3.cloned.1.call-done, s32[2048]{0:T(1024)S(1)} %broadcast_clamp_fusion), kind=kCustom, calls=%fused_computation.1.clone | custom fusion | bytes 4202496 | tf_op jit(solution)/shard_map/jit(_take)/gather | solution.py:46
  108.2 16.7 %gather_fusion = f32[2048,2,128]{2,1,0:T(2,128)} fusion(f32[2,128,4096]{1,0,2:T(2,128)} %all-gather.3.cloned.1.call-done, s32[2048]{0:T(1024)S(1)} %broadcast_clamp_fusion.1), kind=kCustom, calls=%fused_computation.clone | custom fusion | bytes 4202496 | tf_op jit(solution)/shard_map/jit(_take)/gather | solution.py:46
  124.9 7.4 %select_bitcast_fusion = f32[2,128,2048]{1,0,2:T(2,128)S(1)} fusion(f32[2048,2,128]{2,1,0:T(2,128)S(1)} %gather_fusion.1, pred[2048]{0:T(1024)(128)(4,1)S(1)} %compare_and_fusion), kind=kLoop, calls=%fused_computation.8 | loop fusion | flops 524288 | bytes 4196352 | tf_op jit(solution)/shard_map/jit(_take)/select_n | solution.py:46
  134.0 7.4 %select_bitcast_fusion.1 = f32[2,128,2048]{1,0,2:T(2,128)S(1)} fusion(f32[2048,2,128]{2,1,0:T(2,128)S(1)} %copy-done.1, pred[2048]{0:T(1024)(128)(4,1)S(1)} %compare_and_fusion.1), kind=kLoop, calls=%fused_computation.9 | loop fusion | flops 524288 | bytes 4196352 | tf_op jit(solution)/shard_map/jit(_take)/select_n | solution.py:46
  141.5 2.5 fusion.67
  144.0 102.6 %all-gather.5.cloned.1.call-done = f32[2,2048,512]{2,1,0:T(8,128)} async-done(((f32[2,64,512]{2,1,0:T(8,128)}), f32[2,2048,512]{2,1,0:T(8,128)}) %all-gather.5.cloned.1.call-update) | async-done | bytes 8388624 | tf_op jit(solution)/shard_map/all_gather | solution.py:31
  246.6 4.1 slice_multiply_fusion.1
  254.8 1.9 fusion.1
  256.6 1.9 fusion.2
  258.6 1.9 fusion.23
  260.5 1.9 fusion.21
  262.4 2.1 fusion.7
  264.5 1.9 fusion.8
  266.3 1.9 fusion.19
  268.2 1.9 fusion.17
  274.9 343.3 %all-reduce.2.cloned.1.call-done = f32[2,256,512]{1,2,0:T(8,128)} async-done(((f32[2,256,512]{1,2,0:T(8,128)}), f32[2,256,512]{1,2,0:T(8,128)}) %all-reduce.2.cloned.1.call-update) | async-done | bytes 1048592 | tf_op jit(solution)/shard_map/psum | solution.py:71
  (41 shorter events, 18.2 us)
Async XLA Ops:
  7.2 92.1 %all-gather.3.cloned.1.call-start = ((), (), s32[]{:S(2)}) async-start(), calls=%async_computation | async-start | bytes 4456448 | tf_op jit(solution)/shard_map/all_gather | solution.py:30
  9.0 237.5 %all-gather.5.cloned.1.call-start = ((), (), s32[]{:S(2)}) async-start(), calls=%async_computation.1 | async-start | bytes 8650752 | tf_op jit(solution)/shard_map/all_gather | solution.py:31
  9.8 608.4 %all-reduce.2.cloned.1.call-start = ((), (), s32[]{:S(2)}) async-start(), calls=%async_computation.2 | async-start | bytes 2097152 | tf_op jit(solution)/shard_map/psum | solution.py:71
  132.3 1.7 copy-start.1
  254.8 1.9 copy-start
  270.1 3.0 copy-start.2
  273.1 1.5 copy-start.3
Sparse Core Ops, SparseCore 0:
  10.6 88.5 all-gather.2
  102.5 144.0 all-gather.4
  274.8 343.3 all-reduce.1
where the time goes:
time: 627 us
  waiting for transfers between devices  500 us (80%)
  other arithmetic  54.8 us (9%)
  local copies, waits for them, and re-layouts  35.5 us (6%)
  matrix products  22.6 us (4%)
  between operations  14.1 us (2%)
    psum x1, waiting for transfers between devices, on_device(): total_sum = lax.psum(partial_diag, 'row')  343 us
    all_gather x1, waiting for transfers between devices, on_device(): section = lax.all_gather(panel, 'row', axis=1, tiled=True)  103 us
    all_gather x1, waiting for transfers between devices, on_device(): top_strip = lax.all_gather(top_inverse, 'col', axis=2, tiled=True)  52.9 us
    gather x2, local copies, waits for them, and re-layouts, on_device(): picked = jnp.take(top_strip, columns, axis=2)  25.6 us
    dot_general x20, matrix products, product_highest(): jnp.dot(left, right, precision=lax.Precision.HIGHEST, preferred_element_t...  22.6 us
    select_n x2, other arithmetic, on_device(): picked = jnp.take(top_strip, columns, axis=2)  14.9 us
  transfers between devices with their start and end apart: 3, of which 3 were waited for; matrix products, arithmetic and copies ran while one was open for 13% of the time, Pallas kernels for 0%

commit v1 on v0

--- a/solution.py
+++ b/solution.py
@@ -27,7 +27,9 @@
     active_slots = jnp.arange(slot_count, dtype=jnp.int32)[None, :] < leaf_counts[:, None]
     block_live = jnp.any((leaf_rows == my_block) & active_slots, axis=1)
     targets = jnp.arange(ROW_DEV, dtype=jnp.int32)
-    top_strip = lax.all_gather(top_inverse, "col", axis=2, tiled=True)
+    top_strip = jnp.concatenate(
+        lax.all_to_all(jnp.stack([top_inverse] * lax.axis_size("col")), "col", 0, 0), axis=2
+    )
     section = lax.all_gather(panel, "row", axis=1, tiled=True)
     length = section.shape[1]
     gains_prod = []

time: 627 us -> 633 us (level)
  waiting for transfers between devices: 500 us -> 477 us
  local copies, waits for them, and re-layouts: 35.5 us -> 54.2 us
  starting transfers between devices: 0.12 us -> 9.44 us
    all_gather x1, waiting for transfers between devices: 103 us -> 15.4 us  [on_device(): section = lax.all_gather(panel, 'row', axis=1, tiled=True)]
    all_to_all x0 -> x1, waiting for transfers between devices: none -> 60 us  [on_device(): lax.all_to_all(jnp.stack([top_inverse] * lax.axis_size('col')), 'col', 0, 0)]
    psum x1, waiting for transfers between devices: 343 us -> 401 us  [on_device(): total_sum = lax.psum(partial_diag, 'row')]
    all_gather x1 -> x0, waiting for transfers between devices: 52.9 us -> none  [on_device(): top_strip = lax.all_gather(top_inverse, 'col', axis=2, tiled=True)]
    reshape x0 -> x1, local copies, waits for them, and re-layouts: none -> 16.2 us  [on_device(): jnp.concatenate(lax.all_to_all(jnp.stack([top_inverse] * lax.axis_size('c...]
    all_to_all x0 -> x1, starting transfers between devices: none -> 9.36 us  [on_device(): lax.all_to_all(jnp.stack([top_inverse] * lax.axis_size('col')), 'col', 0, 0)]
  transfers between devices with their start and end apart: 3 -> 3, of which waited for: 3 -> 3; matrix products, arithmetic and copies ran while one was open for 13% -> 15% of each run, Pallas kernels for 0% -> 0%
where the time goes in v1:
time: 633 us; the launch traced here: 632 us
  waiting for transfers between devices  477 us (75%)
  local copies, waits for them, and re-layouts  54.2 us (9%)
  other arithmetic  54.2 us (9%)
  matrix products  22.6 us (4%)
  between operations  14.4 us (2%)
  starting transfers between devices  9.44 us (1%)
    psum x1, waiting for transfers between devices, on_device(): total_sum = lax.psum(partial_diag, 'row')  401 us
    all_to_all x1, waiting for transfers between devices, on_device(): lax.all_to_all(jnp.stack([top_inverse] * lax.axis_size('col')), 'col', 0, 0)  60 us
    gather x2, local copies, waits for them, and re-layouts, on_device(): picked = jnp.take(top_strip, columns, axis=2)  25.5 us
    dot_general x20, matrix products, product_highest(): jnp.dot(left, right, precision=lax.Precision.HIGHEST, preferred_element_t...  22.6 us
    reshape x1, local copies, waits for them, and re-layouts, on_device(): jnp.concatenate(lax.all_to_all(jnp.stack([top_inverse] * lax.axis_size('c...  16.2 us
    all_gather x1, waiting for transfers between devices, on_device(): section = lax.all_gather(panel, 'row', axis=1, tiled=True)  15.4 us
    select_n x2, other arithmetic, on_device(): picked = jnp.take(top_strip, columns, axis=2)  14.9 us
  transfers between devices with their start and end apart: 3, of which 3 were waited for; matrix products, arithmetic and copies ran while one was open for 15% of the time, Pallas kernels for 0%

profile of v1, /device:TPU:1, one launch (start us, length us, event | category | flops | bytes accessed | tf_op | source)
XLA Modules:
  0.0 631.9 jit_solution(2056240660681575497)
XLA Ops:
  8.2 2.4 stack.26
  10.6 9.4 %all-to-all-start = ((f32[16,2,128,256]{2,3,1,0:T(8,128)}), f32[16,2,128,256]{2,3,1,0:T(8,128)}, u32[]{:S(2)}, u32[]{:S(2)}) async-start(f32[16,2,128,256]{2,3,1,0:T(8,128)} %stack.26), calls=%async_computation | async-start | bytes 8388608 | tf_op jit(solution)/shard_map/all_to_all | solution.py:31
  21.8 5.0 compare_and_fusion.1
  27.5 5.6 compare_and_fusion.3
  33.1 5.0 compare_and_fusion
  38.2 5.7 compare_and_fusion.2
  43.8 5.0 broadcast_clamp_fusion
  48.9 5.0 broadcast_clamp_fusion.1
  55.2 60.0 %all-to-all-done = f32[16,2,128,256]{2,3,1,0:T(8,128)} async-done(((f32[16,2,128,256]{2,3,1,0:T(8,128)}), f32[16,2,128,256]{2,3,1,0:T(8,128)}, u32[]{:S(2)}, u32[]{:S(2)}) %all-to-all-start) | async-done | bytes 4194336 | tf_op jit(solution)/shard_map/all_to_all | solution.py:31
  115.1 2.5 copy.15
  117.6 16.2 %copy.16 = f32[2,128,4096]{1,0,2:T(2,128)} copy(f32[2,128,4096]{1,2,0:T(8,128)S(1)} %bitcast.120) | data formatting | bytes 8388608 | tf_op jit(solution)/shard_map/reshape | solution.py:30
  133.8 9.0 %gather_fusion.1 = f32[2048,2,128]{2,1,0:T(2,128)S(1)} fusion(f32[2,128,4096]{1,0,2:T(2,128)} %copy.16, s32[2048]{0:T(1024)S(1)} %broadcast_clamp_fusion), kind=kCustom, calls=%fused_computation.1.clone | custom fusion | bytes 4202496 | tf_op jit(solution)/shard_map/jit(_take)/gather | solution.py:48
  142.8 16.6 %gather_fusion = f32[2048,2,128]{2,1,0:T(2,128)} fusion(f32[2,128,4096]{1,0,2:T(2,128)} %copy.16, s32[2048]{0:T(1024)S(1)} %broadcast_clamp_fusion.1), kind=kCustom, calls=%fused_computation.clone | custom fusion | bytes 4202496 | tf_op jit(solution)/shard_map/jit(_take)/gather | solution.py:48
  159.3 7.4 %select_bitcast_fusion = f32[2,128,2048]{1,0,2:T(2,128)S(1)} fusion(f32[2048,2,128]{2,1,0:T(2,128)S(1)} %gather_fusion.1, pred[2048]{0:T(1024)(128)(4,1)S(1)} %compare_and_fusion), kind=kLoop, calls=%fused_computation.8 | loop fusion | flops 524288 | bytes 4196352 | tf_op jit(solution)/shard_map/jit(_take)/select_n | solution.py:48
  168.5 7.4 %select_bitcast_fusion.1 = f32[2,128,2048]{1,0,2:T(2,128)S(1)} fusion(f32[2048,2,128]{2,1,0:T(2,128)S(1)} %copy-done.1, pred[2048]{0:T(1024)(128)(4,1)S(1)} %compare_and_fusion.1), kind=kLoop, calls=%fused_computation.9 | loop fusion | flops 524288 | bytes 4196352 | tf_op jit(solution)/shard_map/jit(_take)/select_n | solution.py:48
  175.9 2.5 fusion.67
  178.4 15.4 %all-gather.2.cloned.1.call-done = f32[2,2048,512]{2,1,0:T(8,128)} async-done(((f32[2,64,512]{2,1,0:T(8,128)}), f32[2,2048,512]{2,1,0:T(8,128)}) %all-gather.2.cloned.1.call-update) | async-done | bytes 8388624 | tf_op jit(solution)/shard_map/all_gather | solution.py:33
  193.8 4.1 slice_multiply_fusion.1
  203.9 1.9 fusion.2
  205.8 1.9 fusion.23
  207.8 1.9 fusion.21
  209.6 2.1 fusion.7
  213.6 1.9 fusion.19
  222.1 400.9 %all-reduce.2.cloned.1.call-done = f32[2,256,512]{1,2,0:T(8,128)} async-done(((f32[2,256,512]{1,2,0:T(8,128)}), f32[2,256,512]{1,2,0:T(8,128)}) %all-reduce.2.cloned.1.call-update) | async-done | bytes 1048592 | tf_op jit(solution)/shard_map/psum | solution.py:73
  (47 shorter events, 22.7 us)
Async XLA Ops:
  10.6 10.2 %copy-start.4 = (s32[2]{0:T(128)S(1)}, s32[2]{0:T(128)}, u32[]{:S(2)}) copy-start(s32[2]{0:T(128)} %param.12) | copy-start | bytes 28
  10.6 10.2 %copy-start.5 = (s32[2,8]{1,0:T(2,128)S(1)}, s32[2,8]{1,0:T(2,128)}, u32[]{:S(2)}) copy-start(s32[2,8]{1,0:T(2,128)} %param.11) | copy-start | bytes 196
  10.6 104.5 %all-to-all-start = ((f32[16,2,128,256]{2,3,1,0:T(8,128)}), f32[16,2,128,256]{2,3,1,0:T(8,128)}, u32[]{:S(2)}, u32[]{:S(2)}) async-start(f32[16,2,128,256]{2,3,1,0:T(8,128)} %stack.26), calls=%async_computation | async-start | bytes 8388608 | tf_op jit(solution)/shard_map/all_to_all | solution.py:31
  20.0 173.8 %all-gather.2.cloned.1.call-start = ((), (), s32[]{:S(2)}) async-start(), calls=%async_computation.1 | async-start | bytes 8650752 | tf_op jit(solution)/shard_map/all_gather | solution.py:33
  20.8 602.3 %all-reduce.2.cloned.1.call-start = ((), (), s32[]{:S(2)}) async-start(), calls=%async_computation.2 | async-start | bytes 2097152 | tf_op jit(solution)/shard_map/psum | solution.py:73
  166.8 1.7 copy-start.1
  202.0 1.9 copy-start
  217.4 3.0 copy-start.2
  220.3 1.5 copy-start.3
Sparse Core Ops, SparseCore 0:
  24.1 169.6 all-gather.1
  222.0 400.9 all-reduce.1
